TPU v7x, 32 devices: a whole 2x2x4 slice. The times are simulated.
32 devices in a mesh: member: 8 (over y, x, core), tile: 4 (over z).
Axes of the slice: x: 2, y: 2, z: 4, core: 2. Of those that a mesh axis runs over, the one named last changes fastest.
Arguments:
- node_fine: int32 [8, 12], P('member'), may hold values from 0 to 8
- node_coarse: int32 [32, 12], P('member'), may hold values from 0 to 8
- weight_fine: int32 [8], P('member'), may hold values from -3 to 3
- weight_coarse: int32 [32], P('member'), may hold values from -3 to 3
- mode_x: float32 [12, 64], replicated, may hold values from -1 to 1
- mode_y: float32 [12, 512], replicated, may hold values from -1 to 1
- mode_z: float32 [12, 32], replicated, may hold values from -1 to 1
- source_fine: float32 [64, 32, 512], P('tile'), may hold values from -12 to 12
- source_coarse: float32 [32, 16, 256], P(None, None, 'tile'), may hold values from -6 to 6
Outputs:
- combined: float32 [32, 16, 256], P('member', None, 'tile')
All inputs are finite; a program needn't handle non-finite values.
Results may differ from a plain program's by a relative error of at most 0.00026.
Values sent between devices are 32-bit elements; how exact they have to be, the bound alone decides.
No kernel may reach another device: no remote copies, remote signals or barrier semaphores. Data moves between devices by JAX's collectives and lax.ppermute only.
A program may use at most 192 MiB of HBM per device.

v0:
```python
import math
import jax
import jax.numpy as jnp
from jax import lax
from jax.sharding import PartitionSpec as P

NODES = 9
SWEEPS = 3
CENTRE = 1.125
HALF_WIDTH = 0.875
SPREAD_RATIO = CENTRE / HALF_WIDTH


def extended(block, sides, width):
    for axis, dim in sides:
        count = lax.axis_size(axis)
        forward = [(i, i + 1) for i in range(count - 1)]
        backward = [(target, source) for source, target in forward]
        low = lax.ppermute(
            lax.slice_in_dim(block, block.shape[dim] - width, None, axis=dim), axis, forward
        )
        high = lax.ppermute(lax.slice_in_dim(block, 0, width, axis=dim), axis, backward)
        block = jnp.concatenate([low, block, high], axis=dim)
    return block


def sweep_factors(sweep_count):
    previous = 1.0 / SPREAD_RATIO
    factors = []
    for _ in range(sweep_count - 1):
        current = 1.0 / (2.0 * SPREAD_RATIO - previous)
        factors.append((current * previous, 2.0 * current / HALF_WIDTH))
        previous = current
    return factors


def shifted(tensor, spatial, along_dim, offset):
    for current in spatial:
        begin_at = offset if current == along_dim else 1
        tensor = lax.slice_in_dim(
            tensor, begin_at, tensor.shape[current] - 2 + begin_at, axis=current
        )
    return tensor


def diagonal_of(cond_pad, spatial):
    centre = shifted(cond_pad, spatial, -1, 1)
    running = jnp.zeros_like(centre)
    for along_dim in spatial:
        for offset in (0, 2):
            running = running + 0.5 * (centre + shifted(cond_pad, spatial, along_dim, offset))
    return running


def apply_op(field_pad, cond_pad, spatial):
    centre_k = shifted(cond_pad, spatial, -1, 1)
    centre_v = shifted(field_pad, spatial, -1, 1)
    running = jnp.zeros_like(centre_v * centre_k)
    for along_dim in spatial:
        for offset in (0, 2):
            coupling = 0.5 * (centre_k + shifted(cond_pad, spatial, along_dim, offset))
            running = running + coupling * (
                centre_v - shifted(field_pad, spatial, along_dim, offset)
            )
    return running


def node_values(node_index):
    return jnp.cos(math.pi * node_index.astype(jnp.float32) / (NODES - 1))


def pair_mean(modes):
    return 0.5 * (modes[:, 0::2] + modes[:, 1::2])


def log_field(values, along_x, along_z, along_y):
    weighted = (along_x.T * values)[:, None, :] * along_z.T[None, :, :]
    flattened = weighted.reshape(weighted.shape[0] * weighted.shape[1], weighted.shape[2])
    product = jnp.dot(flattened, along_y, precision=lax.Precision.HIGHEST)
    return product.reshape(weighted.shape[0], weighted.shape[1], along_y.shape[1])


def log_batch(values, along_x, along_z, along_y):
    weighted = (along_x.T[None, :, :] * values[:, None, :])[:, :, None, :] * along_z.T[
        None, None, :, :
    ]
    shape_in = weighted.shape
    flattened = weighted.reshape(shape_in[0] * shape_in[1] * shape_in[2], shape_in[3])
    product = jnp.dot(flattened, along_y, precision=lax.Precision.HIGHEST)
    return product.reshape(shape_in[0], shape_in[1], shape_in[2], along_y.shape[1])


def restrict(tensor):
    blocks = tensor.reshape(
        tensor.shape[0] // 2, 2, tensor.shape[1] // 2, 2, tensor.shape[2] // 2, 2
    )
    return blocks.sum(axis=(1, 3, 5)) * 0.125


def trim_dim(tensor, trim_depth, along_dim):
    return lax.slice_in_dim(
        tensor, trim_depth, tensor.shape[along_dim] - trim_depth, axis=along_dim
    )


def pad_other(tensor, halo_dim, spatial):
    widths = []
    for position in range(tensor.ndim):
        if position in spatial and position != halo_dim:
            widths.append((1, 1))
        else:
            widths.append((0, 0))
    return jnp.pad(tensor, widths)


def smooth_deep(source_ext, cond_pad, halo_dim, spatial, inside, reach_cells, factors):
    diagonal = diagonal_of(cond_pad, spatial)
    safe_diag = diagonal + (1.0 - inside)
    update = source_ext / (CENTRE * safe_diag) * inside
    result = trim_dim(update, reach_cells, halo_dim)
    residual = source_ext
    extent = reach_cells
    for keep_part, push_part in factors:
        cond_part = trim_dim(cond_pad, reach_cells + 1 - extent, halo_dim)
        applied = apply_op(pad_other(update, halo_dim, spatial), cond_part, spatial)
        residual = trim_dim(residual, 1, halo_dim) - applied
        extent = extent - 1
        trim_depth = reach_cells - extent
        fresh = keep_part * trim_dim(update, 1, halo_dim) + push_part * residual / trim_dim(
            safe_diag, trim_depth, halo_dim
        )
        update = fresh * trim_dim(inside, trim_depth, halo_dim)
        result = result + trim_dim(update, extent, halo_dim)
    return result


def body(
    node_fine,
    node_coarse,
    weight_fine,
    weight_coarse,
    mode_x,
    mode_y,
    mode_z,
    source_fine,
    source_coarse,
):
    factors = sweep_factors(SWEEPS)
    reach_cells = SWEEPS - 1
    tile_place = lax.axis_index("tile")
    strip_width = source_fine.shape[0]
    coarse_width = source_coarse.shape[2]
    mode_xc = pair_mean(mode_x)
    mode_yc = pair_mean(mode_y)
    mode_zc = pair_mean(mode_z)
    extent = reach_cells + 1
    padded_x = jnp.pad(mode_x, ((0, 0), (extent, extent)))
    mode_slab = lax.dynamic_slice_in_dim(
        padded_x, tile_place * strip_width, strip_width + 2 * extent, 1
    )
    global_x = (
        tile_place * strip_width - extent + jnp.arange(strip_width + 2 * extent, dtype=jnp.int32)
    )
    inside_x = ((global_x >= 0) & (global_x < mode_x.shape[1])).astype(jnp.float32)
    conduct = (
        jnp.exp(log_field(node_values(node_fine[0]), mode_slab, mode_z, mode_y))
        * inside_x[:, None, None]
    )
    cond_fine = pad_other(conduct, 0, (0, 1, 2))
    padded_y = jnp.pad(mode_yc, ((0, 0), (extent, extent)))
    mode_strip = lax.dynamic_slice_in_dim(
        padded_y, tile_place * coarse_width, coarse_width + 2 * extent, 1
    )
    global_y = (
        tile_place * coarse_width - extent + jnp.arange(coarse_width + 2 * extent, dtype=jnp.int32)
    )
    inside_y = ((global_y >= 0) & (global_y < mode_yc.shape[1])).astype(jnp.float32)
    conduct_c = (
        jnp.exp(log_batch(node_values(node_coarse), mode_xc, mode_zc, mode_strip)) * inside_y
    )
    cond_coarse = pad_other(conduct_c, 3, (1, 2, 3))
    fine_ext = extended(source_fine, (("tile", 0),), reach_cells)
    fine_inside = trim_dim(inside_x, 1, 0)[:, None, None]
    fine_result = smooth_deep(fine_ext, cond_fine, 0, (0, 1, 2), fine_inside, reach_cells, factors)
    coarse_ext = extended(source_coarse, (("tile", 2),), reach_cells)
    coarse_inside = trim_dim(inside_y, 1, 0)[None, None, None, :]
    coarse_result = smooth_deep(
        coarse_ext[None], cond_coarse, 3, (1, 2, 3), coarse_inside, reach_cells, factors
    )
    fine_part = weight_fine[0].astype(jnp.float32) * restrict(fine_result)
    arrived = lax.all_to_all(fine_part, "tile", split_axis=2, concat_axis=0, tiled=True)
    coarse_part = jnp.tensordot(
        weight_coarse.astype(jnp.float32), coarse_result, axes=1, precision=lax.Precision.HIGHEST
    )
    summed = arrived + coarse_part
    return lax.psum_scatter(summed, "member", scatter_dimension=0, tiled=True)


def solution(mesh):
    return jax.shard_map(
        body,
        mesh=mesh,
        in_specs=(
            P("member", None),
            P("member", None),
            P("member"),
            P("member"),
            P(),
            P(),
            P(),
            P("tile", None, None),
            P(None, None, "tile"),
        ),
        out_specs=P("member", None, "tile"),
        check_vma=False,
    )
```

profile of v0, /device:TPU:0, one launch (start us, length us, event | category | flops | bytes accessed | tf_op | source)
XLA Modules:
  0.0 194.3 jit_solution(10056728130827275311)
XLA Ops:
  6.5 1.7 fusion.159
  8.3 5.6 %collective-permute-start = (f32[2,32,512]{2,1,0:T(8,128)}, f32[2,32,512]{2,1,0:T(8,128)}, u32[]{:S(2)}, u32[]{:S(2)}) collective-permute-start(f32[2,32,512]{2,1,0:T(8,128)} %get-tuple-element.14), channel_id=1, source_target_pairs={{0,1},{1,2},{2,3},{4,5},{5,6},{6,7},{8,9},{9,10},{10,11},{12,13},{... | collective-permute-start | bytes 393224 | tf_op jit(solution)/shard_map/ppermute | solution.py:19
  13.9 1.3 collective-permute-start.1
  15.2 1.2 fusion.160
  16.3 4.6 %collective-permute-start.2 = (f32[32,16,2]{2,1,0:T(8,128)S(1)}, f32[32,16,2]{2,1,0:T(8,128)S(1)}, u32[]{:S(2)}, u32[]{:S(2)}) collective-permute-start(f32[32,16,2]{2,1,0:T(8,128)S(1)} %get-tuple-element.15), channel_id=1, source_target_pairs={{0,1},{1,2},{2,3},{4,5},{5,6},{6,7},{8,9},{9,10},{10,11},{12,13},{... | collective-permute-start | bytes 12296 | tf_op jit(solution)/shard_map/ppermute | solution.py:19
  20.9 1.3 collective-permute-start.3
  22.2 0.1 slice.637
  22.4 0.1 slice.638
  22.5 0.5 slice.641
  23.0 0.5 slice.642
  23.5 0.1 slice.639
  23.6 0.1 slice.640
  23.8 0.1 multiply_bitcast_fusion.2
  23.9 0.1 copy.29
  24.0 0.1 broadcast_subtract_fusion.1
  24.1 0.1 copy.34
  24.3 0.1 slice_bitcast_fusion.2
  24.3 1.7 fusion
  26.1 0.1 broadcast_multiply_fusion.1
  26.2 1.9 fusion.1
  29.0 1.0 collective-permute-done.3
  30.0 0.2 pad_maximum_fusion
  30.2 0.1 copy.33
  30.3 0.2 fusion.161
  30.5 0.1 slice_bitcast_fusion
  30.7 0.1 copy.35
  30.8 1.7 divide_multiply_fusion.1
  32.5 4.2 %fusion.128 = (f32[4,32,16,66]{3,1,2,0:T(8,128)S(1)}, f32[4,32,16,66]{3,1,2,0:T(8,128)S(1)}) fusion(f32[4,32,16,68]{3,1,2,0:T(8,128)S(1)} %get-tuple-element.12, f32[4,32,16,68]{3,1,2,0:T(8,128)S(1)} %get-tuple-element.11, f32[66]{0:T(128)S(1)} %slice_bitcast_fusion.2, f32[4,32,16,70]{3,1,2,0:T(8,128)S(1)} %fusion.1, f32[32,16,66]{2,0,1:T(8,128)S(1)} %copy.35), kind=kLoop, calls=%fused_computation.183 | loop fusion | flops 4730880 | bytes 10781184 | tf_op jit(solution)/shard_map/mul | solution.py:132
  36.7 4.5 %fusion.133 = f32[4,32,16,64]{3,1,2,0:T(8,128)S(1)} fusion(f32[4,32,16,68]{3,1,2,0:T(8,128)S(1)} %get-tuple-element.11, f32[4,32,16,68]{3,1,2,0:T(8,128)S(1)} %get-tuple-element.12, f32[4,32,16,66]{3,1,2,0:T(8,128)S(1)} %get-tuple-element.9, f32[4,32,16,70]{3,1,2,0:T(8,128)S(1)} %fusion.1, f32[4,32,16,66]{3,1,2,0:T(8,128)S(1)} %get-tuple-element.10, ...), kind=kLoop, calls=%fused_computation.193 | loop fusion | flops 4849664 | bytes 12059136 | tf_op jit(solution)/shard_map/add | solution.py:133
  41.2 0.9 constant_dynamic-update-slice_fusion.2
  42.2 0.1 constant_dynamic-update-slice_fusion.1
  42.3 0.9 constant_dynamic-update-slice_fusion
  43.2 1.2 divide_multiply_fusion
  44.4 2.9 %fusion.35 = (f32[18,32,512]{2,1,0:T(8,128)S(1)}, f32[18,32,512]{2,1,0:T(8,128)S(1)}) fusion(f32[20,32,512]{2,1,0:T(8,128)S(1)} %get-tuple-element.8, f32[20,32,512]{2,1,0:T(8,128)S(1)} %get-tuple-element.7, f32[18]{0:T(128)S(1)} %slice.617, f32[22,32,512]{2,1,0:T(8,128)S(1)} %fusion, f32[20,32,512]{2,1,0:T(8,128)S(1)} %constant_dynamic-update-slice_fusion), kind=kLoop, calls=%fused_computation.81 | loop fusion | flops 10321920 | bytes 14549504 | tf_op jit(solution)/shard_map/mul | solution.py:132
  47.3 2.7 %fusion.139 = f32[16,32,512]{2,1,0:T(8,128)S(1)} fusion(f32[20,32,512]{2,1,0:T(8,128)S(1)} %get-tuple-element.7, f32[20,32,512]{2,1,0:T(8,128)S(1)} %get-tuple-element.8, f32[18,32,512]{2,1,0:T(8,128)S(1)} %get-tuple-element.5, f32[22,32,512]{2,1,0:T(8,128)S(1)} %fusion, f32[18,32,512]{2,1,0:T(8,128)S(1)} %get-tuple-element.6, f32[16]{0:T(128)S(1)} %slice.634), kind=kLoop, calls=%fused_computation.206 | loop fusion | flops 9699328 | bytes 13107712 | tf_op jit(solution)/shard_map/add | solution.py:133
  50.0 68.4 %reshape.50 = f32[8,2,16,2,256,2]{5,4,3,2,1,0:T(8,128)} reshape(f32[16,32,512]{2,1,0:T(8,128)S(1)} %fusion.139) | data formatting | bytes 2097152 | tf_op jit(solution)/shard_map/reshape | solution.py:94
  118.4 20.8 %reduce_sum.9 = f32[8,16,256]{2,1,0:T(8,128)S(1)} reduce(f32[8,2,16,2,256,2]{5,4,3,2,1,0:T(8,128)} %reshape.50, f32[]{:T(128)} %constant.18.clone.1), dimensions={1,3,5}, to_apply=%region_0.1 | reduce | flops 229376 | bytes 1179652 | tf_op jit(solution)/shard_map/reduce_sum | solution.py:97
  139.2 0.4 copy.30
  139.6 1.0 reshape.55
  140.7 4.9 %all-to-all-start = ((f32[4,1,8192]{2,1,0:T(1,128)}), f32[4,1,8192]{2,1,0:T(1,128)S(1)}, u32[]{:S(2)}, u32[]{:S(2)}) async-start(f32[4,1,8192]{2,1,0:T(1,128)} %reshape.55), calls=%async_computation | async-start | bytes 262144 | tf_op jit(solution)/shard_map/all_to_all | solution.py:191
  145.6 2.6 %fusion.140 = f32[1,32,16,64]{3,0,2,1:T(1,128)S(1)} fusion(f32[4,32,16,64]{3,1,2,0:T(8,128)S(1)} %fusion.133, s32[4]{0:T(128)S(1)} %copy-done.6), kind=kOutput, calls=%fused_computation.207 | convolution fusion | flops 1572868 | bytes 655376 | tf_op jit(solution)/shard_map/dot_general | solution.py:192
  148.1 3.3 %all-to-all-done = f32[4,1,8192]{2,1,0:T(1,128)S(1)} async-done(((f32[4,1,8192]{2,1,0:T(1,128)}), f32[4,1,8192]{2,1,0:T(1,128)S(1)}, u32[]{:S(2)}, u32[]{:S(2)}) %all-to-all-start) | async-done | bytes 131104 | tf_op jit(solution)/shard_map/all_to_all | solution.py:191
  151.5 0.5 broadcast.125
  152.0 1.0 reduce
  153.0 0.4 reshape.56
  153.4 0.4 copy.40
  153.8 0.7 bitcast_add_fusion
  154.6 32.9 %reduce-scatter.2.cloned.1.call-done = f32[4,16,64]{2,1,0:T(8,128)} async-done(((f32[32,16,64]{2,1,0:T(8,128)}), f32[4,16,64]{2,1,0:T(8,128)}) %reduce-scatter.2.cloned.1.call-update) | async-done | bytes 16400 | tf_op jit(solution)/shard_map/reduce_scatter | solution.py:196
  (34 shorter events, 0.5 us)
Async XLA Ops:
  6.5 15.7 %copy-start.4 = (f32[12,64]{1,0:T(8,128)S(1)}, f32[12,64]{1,0:T(8,128)}, u32[]{:S(2)}) copy-start(f32[12,64]{1,0:T(8,128)} %param.13) | copy-start | bytes 9220
  6.5 16.0 %copy-start.2 = (f32[12,512]{1,0:T(8,128)S(1)}, f32[12,512]{1,0:T(8,128)}, u32[]{:S(2)}) copy-start(f32[12,512]{1,0:T(8,128)} %param.14) | copy-start | bytes 73732
  6.5 17.0 %copy-start.3 = (f32[12,32]{1,0:T(8,128)S(1)}, f32[12,32]{1,0:T(8,128)}, u32[]{:S(2)}) copy-start(f32[12,32]{1,0:T(8,128)} %param.15) | copy-start | bytes 4612
  6.5 17.2 %copy-start.7 = (s32[1,12]{1,0:T(1,128)S(1)}, s32[1,12]{1,0:T(1,128)}, u32[]{:S(2)}) copy-start(s32[1,12]{1,0:T(1,128)} %param.9) | copy-start | bytes 148
  6.5 17.5 %copy-start.5 = (s32[4,12]{1,0:T(4,128)S(1)}, s32[4,12]{1,0:T(4,128)}, u32[]{:S(2)}) copy-start(s32[4,12]{1,0:T(4,128)} %param.10) | copy-start | bytes 580
  8.3 32.9 %collective-permute-start = (f32[2,32,512]{2,1,0:T(8,128)}, f32[2,32,512]{2,1,0:T(8,128)}, u32[]{:S(2)}, u32[]{:S(2)}) collective-permute-start(f32[2,32,512]{2,1,0:T(8,128)} %get-tuple-element.14), channel_id=1, source_target_pairs={{0,1},{1,2},{2,3},{4,5},{5,6},{6,7},{8,9},{9,10},{10,11},{12,13},{... | collective-permute-start | bytes 393224 | tf_op jit(solution)/shard_map/ppermute | solution.py:19
  13.9 28.4 %collective-permute-start.1 = (f32[2,32,512]{2,1,0:T(8,128)}, f32[2,32,512]{2,1,0:T(8,128)}, u32[]{:S(2)}, u32[]{:S(2)}) collective-permute-start(f32[2,32,512]{2,1,0:T(8,128)} %get-tuple-element.13), channel_id=1, source_target_pairs={{1,0},{2,1},{3,2},{5,4},{6,5},{7,6},{9,8},{10,9},{11,10},{13,12},{... | collective-permute-start | bytes 393224 | tf_op jit(solution)/shard_map/ppermute | solution.py:22
  16.3 12.6 %collective-permute-start.2 = (f32[32,16,2]{2,1,0:T(8,128)S(1)}, f32[32,16,2]{2,1,0:T(8,128)S(1)}, u32[]{:S(2)}, u32[]{:S(2)}) collective-permute-start(f32[32,16,2]{2,1,0:T(8,128)S(1)} %get-tuple-element.15), channel_id=1, source_target_pairs={{0,1},{1,2},{2,3},{4,5},{5,6},{6,7},{8,9},{9,10},{10,11},{12,13},{... | collective-permute-start | bytes 12296 | tf_op jit(solution)/shard_map/ppermute | solution.py:19
  20.9 9.1 %collective-permute-start.3 = (f32[32,16,2]{2,1,0:T(8,128)S(1)}, f32[32,16,2]{2,1,0:T(8,128)S(1)}, u32[]{:S(2)}, u32[]{:S(2)}) collective-permute-start(f32[32,16,2]{2,1,0:T(8,128)S(1)} %get-tuple-element.16), channel_id=1, source_target_pairs={{1,0},{2,1},{3,2},{5,4},{6,5},{7,6},{9,8},{10,9},{11,10},{13,12},{... | collective-permute-start | bytes 12296 | tf_op jit(solution)/shard_map/ppermute | solution.py:22
  24.3 5.7 %copy-start = (f32[32,16,64]{2,1,0:T(8,128)S(1)}, f32[32,16,64]{2,1,0:T(8,128)}, u32[]{:S(2)}) copy-start(f32[32,16,64]{2,1,0:T(8,128)} %param.17) | copy-start | bytes 393220
  36.7 5.5 %copy-start.1 = (f32[16,32,512]{2,1,0:T(8,128)S(1)}, f32[16,32,512]{2,1,0:T(8,128)}, u32[]{:S(2)}) copy-start(f32[16,32,512]{2,1,0:T(8,128)} %param.16) | copy-start | bytes 3145732
  139.2 6.4 %copy-start.6 = (s32[4]{0:T(128)S(1)}, s32[4]{0:T(128)}, u32[]{:S(2)}) copy-start(s32[4]{0:T(128)} %param.12) | copy-start | bytes 52
  140.7 10.8 %all-to-all-start = ((f32[4,1,8192]{2,1,0:T(1,128)}), f32[4,1,8192]{2,1,0:T(1,128)S(1)}, u32[]{:S(2)}, u32[]{:S(2)}) async-start(f32[4,1,8192]{2,1,0:T(1,128)} %reshape.55), calls=%async_computation | async-start | bytes 262144 | tf_op jit(solution)/shard_map/all_to_all | solution.py:191
  145.6 41.9 %reduce-scatter.2.cloned.1.call-start = ((), (), s32[]{:S(2)}) async-start(), calls=%async_computation.2 | async-start | bytes 294912 | tf_op jit(solution)/shard_map/reduce_scatter | solution.py:196
Sparse Core Ops, SparseCore 0:
  154.7 32.7 reduce-scatter.1
where the time goes:
time: 195 us; the launch traced here: 194 us
  local copies, waits for them, and re-layouts  78.2 us (40%)
  other arithmetic  40.5 us (21%)
  waiting for transfers between devices  37.3 us (19%)
  starting transfers between devices  17.7 us (9%)
  between operations  14.4 us (7%)
  matrix products  6.21 us (3%)
    reshape x1, local copies, waits for them, and re-layouts, restrict(): tensor.reshape(tensor.shape[0] // 2, 2, tensor.shape[1] // 2, 2, tensor.s...  68.4 us
    reduce_scatter x1, waiting for transfers between devices, body(): return lax.psum_scatter(summed, 'member', scatter_dimension=0, tiled=True)  32.9 us
    reduce_sum x1, other arithmetic, restrict(): return blocks.sum(axis=(1, 3, 5)) * 0.125  20.8 us
    ppermute x2, starting transfers between devices, extended(): lax.ppermute(lax.slice_in_dim(block, block.shape[dim] - width, None, axis...  10.2 us
    add x2, other arithmetic, smooth_deep(): result = result + trim_dim(update, extent, halo_dim)  7.19 us
    mul x2, other arithmetic, smooth_deep(): update = fresh * trim_dim(inside, trim_depth, halo_dim)  7.12 us
    all_to_all x1, starting transfers between devices, body(): lax.all_to_all(fine_part, 'tile', split_axis=2, concat_axis=0, tiled=True)  4.92 us
  transfers between devices with their start and end apart: 6, of which 3 were waited for; matrix products, arithmetic and copies ran while one was open for 11% of the time, Pallas kernels for 0%

commit v1 on v0

--- a/solution.py
+++ b/solution.py
@@ -188,7 +188,9 @@
         coarse_ext[None], cond_coarse, 3, (1, 2, 3), coarse_inside, reach_cells, factors
     )
     fine_part = weight_fine[0].astype(jnp.float32) * restrict(fine_result)
-    arrived = lax.all_to_all(fine_part, "tile", split_axis=2, concat_axis=0, tiled=True)
+    arrived = jnp.concatenate(
+        lax.all_to_all(jnp.stack(jnp.split(fine_part, lax.axis_size("tile"), 2)), "tile", 0, 0), 0
+    )
     coarse_part = jnp.tensordot(
         weight_coarse.astype(jnp.float32), coarse_result, axes=1, precision=lax.Precision.HIGHEST
     )

time: 195 us -> 194 us (level)
  no operation moved by 1% of the time
where the time goes in v1:
time: 194 us; the launch traced here: 193 us
  local copies, waits for them, and re-layouts  77 us (40%)
  other arithmetic  40.6 us (21%)
  waiting for transfers between devices  37.3 us (19%)
  starting transfers between devices  17.7 us (9%)
  between operations  14.4 us (7%)
  matrix products  6.2 us (3%)
    reshape x1, local copies, waits for them, and re-layouts, restrict(): tensor.reshape(tensor.shape[0] // 2, 2, tensor.shape[1] // 2, 2, tensor.s...  68.4 us
    reduce_scatter x1, waiting for transfers between devices, body(): return lax.psum_scatter(summed, 'member', scatter_dimension=0, tiled=True)  32.9 us
    reduce_sum x1, other arithmetic, restrict(): return blocks.sum(axis=(1, 3, 5)) * 0.125  20.8 us
    ppermute x2, starting transfers between devices, extended(): lax.ppermute(lax.slice_in_dim(block, block.shape[dim] - width, None, axis...  10.2 us
    add x2, other arithmetic, smooth_deep(): result = result + trim_dim(update, extent, halo_dim)  7.19 us
    mul x2, other arithmetic, smooth_deep(): update = fresh * trim_dim(inside, trim_depth, halo_dim)  7.12 us
    all_to_all x1, starting transfers between devices, body(): lax.all_to_all(jnp.stack(jnp.split(fine_part, lax.axis_size('tile'), 2)),...  4.93 us
  transfers between devices with their start and end apart: 6, of which 3 were waited for; matrix products, arithmetic and copies ran while one was open for 11% of the time, Pallas kernels for 0%

profile of v1, /device:TPU:0, one launch (start us, length us, event | category | flops | bytes accessed | tf_op | source)
XLA Modules:
  0.0 193.2 jit_solution(6014242047671876361)
XLA Ops:
  6.5 1.7 fusion.159
  8.3 5.6 %collective-permute-start = (f32[2,32,512]{2,1,0:T(8,128)}, f32[2,32,512]{2,1,0:T(8,128)}, u32[]{:S(2)}, u32[]{:S(2)}) collective-permute-start(f32[2,32,512]{2,1,0:T(8,128)} %get-tuple-element.14), channel_id=1, source_target_pairs={{0,1},{1,2},{2,3},{4,5},{5,6},{6,7},{8,9},{9,10},{10,11},{12,13},{... | collective-permute-start | bytes 393224 | tf_op jit(solution)/shard_map/ppermute | solution.py:19
  13.9 1.3 collective-permute-start.1
  15.2 1.2 fusion.160
  16.3 4.6 %collective-permute-start.2 = (f32[32,16,2]{2,1,0:T(8,128)S(1)}, f32[32,16,2]{2,1,0:T(8,128)S(1)}, u32[]{:S(2)}, u32[]{:S(2)}) collective-permute-start(f32[32,16,2]{2,1,0:T(8,128)S(1)} %get-tuple-element.15), channel_id=1, source_target_pairs={{0,1},{1,2},{2,3},{4,5},{5,6},{6,7},{8,9},{9,10},{10,11},{12,13},{... | collective-permute-start | bytes 12296 | tf_op jit(solution)/shard_map/ppermute | solution.py:19
  20.9 1.3 collective-permute-start.3
  22.2 0.1 slice.637
  22.4 0.1 slice.638
  22.5 0.5 slice.641
  23.0 0.5 slice.642
  23.5 0.1 slice.639
  23.6 0.1 slice.640
  23.8 0.1 multiply_bitcast_fusion.2
  23.8 0.1 copy.14
  23.9 0.1 broadcast_subtract_fusion.1
  24.1 0.1 copy.16
  24.2 0.1 slice_bitcast_fusion.7
  24.2 0.1 slice_bitcast_fusion.6
  24.3 1.7 fusion
  26.1 0.1 broadcast_multiply_fusion.1
  26.1 1.9 %fusion.1 = f32[4,32,16,70]{3,1,2,0:T(8,128)S(1)} fusion(f32[70]{0:T(128)S(1)} %and_convert_fusion, f32[16,12]{1,0:T(8,128)S(1)} %copy.16, f32[4,32,12]{1,2,0:T(8,128)S(1)} %broadcast_multiply_fusion.1, s32[]{:T(128)S(6)} %select_n.7, f32[12,256]{1,0:T(8,128)S(1)} %add_multiply_fusion), kind=kOutput, calls=%fused_computation.43 | convolution fusion | flops 20811776 | bytes 592924 | tf_op jit(solution)/shard_map/dot_general | solution.py:89
  29.0 1.0 collective-permute-done.3
  30.0 0.2 pad_maximum_fusion.1
  30.2 0.1 copy.15
  30.3 0.2 fusion.161
  30.5 0.1 slice_bitcast_fusion
  30.7 0.1 copy.17
  30.7 1.7 divide_multiply_fusion.1
  32.4 4.2 %fusion.128 = (f32[4,32,16,66]{3,1,2,0:T(8,128)S(1)}, f32[4,32,16,66]{3,1,2,0:T(8,128)S(1)}) fusion(f32[4,32,16,68]{3,1,2,0:T(8,128)S(1)} %get-tuple-element.12, f32[4,32,16,68]{3,1,2,0:T(8,128)S(1)} %get-tuple-element.11, f32[66]{0:T(128)S(1)} %slice_bitcast_fusion.6, f32[4,32,16,70]{3,1,2,0:T(8,128)S(1)} %fusion.1, f32[32,16,66]{2,0,1:T(8,128)S(1)} %copy.17), kind=kLoop, calls=%fused_computation.183 | loop fusion | flops 4730880 | bytes 10781184 | tf_op jit(solution)/shard_map/mul | solution.py:132
  36.7 4.5 %fusion.133 = f32[4,32,16,64]{3,1,2,0:T(8,128)S(1)} fusion(f32[4,32,16,68]{3,1,2,0:T(8,128)S(1)} %get-tuple-element.11, f32[4,32,16,68]{3,1,2,0:T(8,128)S(1)} %get-tuple-element.12, f32[4,32,16,66]{3,1,2,0:T(8,128)S(1)} %get-tuple-element.9, f32[4,32,16,70]{3,1,2,0:T(8,128)S(1)} %fusion.1, f32[4,32,16,66]{3,1,2,0:T(8,128)S(1)} %get-tuple-element.10, ...), kind=kLoop, calls=%fused_computation.193 | loop fusion | flops 4849664 | bytes 12059136 | tf_op jit(solution)/shard_map/add | solution.py:133
  41.2 0.9 constant_dynamic-update-slice_fusion.2
  42.2 0.1 constant_dynamic-update-slice_fusion.1
  42.3 0.9 constant_dynamic-update-slice_fusion
  43.2 1.2 divide_multiply_fusion
  44.4 2.9 %fusion.35 = (f32[18,32,512]{2,1,0:T(8,128)S(1)}, f32[18,32,512]{2,1,0:T(8,128)S(1)}) fusion(f32[20,32,512]{2,1,0:T(8,128)S(1)} %get-tuple-element.8, f32[20,32,512]{2,1,0:T(8,128)S(1)} %get-tuple-element.7, f32[18]{0:T(128)S(1)} %slice.617, f32[22,32,512]{2,1,0:T(8,128)S(1)} %fusion, f32[20,32,512]{2,1,0:T(8,128)S(1)} %constant_dynamic-update-slice_fusion), kind=kLoop, calls=%fused_computation.81 | loop fusion | flops 10321920 | bytes 14549504 | tf_op jit(solution)/shard_map/mul | solution.py:132
  47.3 2.7 %fusion.139 = f32[16,32,512]{2,1,0:T(8,128)S(1)} fusion(f32[20,32,512]{2,1,0:T(8,128)S(1)} %get-tuple-element.7, f32[20,32,512]{2,1,0:T(8,128)S(1)} %get-tuple-element.8, f32[18,32,512]{2,1,0:T(8,128)S(1)} %get-tuple-element.5, f32[22,32,512]{2,1,0:T(8,128)S(1)} %fusion, f32[18,32,512]{2,1,0:T(8,128)S(1)} %get-tuple-element.6, f32[16]{0:T(128)S(1)} %slice.634), kind=kLoop, calls=%fused_computation.206 | loop fusion | flops 9699328 | bytes 13107712 | tf_op jit(solution)/shard_map/add | solution.py:133
  50.0 68.4 %reshape.53 = f32[8,2,16,2,256,2]{5,4,3,2,1,0:T(8,128)} reshape(f32[16,32,512]{2,1,0:T(8,128)S(1)} %fusion.139) | data formatting | bytes 2097152 | tf_op jit(solution)/shard_map/reshape | solution.py:94
  118.4 20.8 %reduce_sum.9 = f32[8,16,256]{2,1,0:T(8,128)S(1)} reduce(f32[8,2,16,2,256,2]{5,4,3,2,1,0:T(8,128)} %reshape.53, f32[]{:T(128)} %constant.18.clone.1), dimensions={1,3,5}, to_apply=%region_0.1 | reduce | flops 229376 | bytes 1179652 | tf_op jit(solution)/shard_map/reduce_sum | solution.py:97
  139.2 0.1 slice_bitcast_fusion.4
  139.3 0.8 reshape.59
  140.2 4.9 %all-to-all-start = ((f32[4,1,8192]{2,1,0:T(1,128)}), f32[4,1,8192]{2,1,0:T(1,128)S(1)}, u32[]{:S(2)}, u32[]{:S(2)}) async-start(f32[4,1,8192]{2,1,0:T(1,128)} %reshape.59), calls=%async_computation | async-start | bytes 262144 | tf_op jit(solution)/shard_map/all_to_all | solution.py:192
  145.1 2.6 %fusion.140 = f32[1,32,16,64]{3,0,2,1:T(1,128)S(1)} fusion(f32[4,32,16,64]{3,1,2,0:T(8,128)S(1)} %fusion.133, s32[4]{0:T(128)S(1)} %copy-done.6), kind=kOutput, calls=%fused_computation.207 | convolution fusion | flops 1572868 | bytes 655376 | tf_op jit(solution)/shard_map/dot_general | solution.py:194
  147.7 3.4 %all-to-all-done = f32[4,1,8192]{2,1,0:T(1,128)S(1)} async-done(((f32[4,1,8192]{2,1,0:T(1,128)}), f32[4,1,8192]{2,1,0:T(1,128)S(1)}, u32[]{:S(2)}, u32[]{:S(2)}) %all-to-all-start) | async-done | bytes 131104 | tf_op jit(solution)/shard_map/all_to_all | solution.py:192
  151.0 0.5 broadcast.125
  151.5 1.0 reduce
  152.5 0.2 reshape.60
  152.7 0.7 bitcast_add_fusion
  153.4 32.9 %reduce-scatter.2.cloned.1.call-done = f32[4,16,64]{2,1,0:T(8,128)} async-done(((f32[32,16,64]{2,1,0:T(8,128)}), f32[4,16,64]{2,1,0:T(8,128)}) %reduce-scatter.2.cloned.1.call-update) | async-done | bytes 16400 | tf_op jit(solution)/shard_map/reduce_scatter | solution.py:198
  (33 shorter events, 0.4 us)
Async XLA Ops:
  6.5 15.7 %copy-start.4 = (f32[12,64]{1,0:T(8,128)S(1)}, f32[12,64]{1,0:T(8,128)}, u32[]{:S(2)}) copy-start(f32[12,64]{1,0:T(8,128)} %param.13) | copy-start | bytes 9220
  6.5 16.0 %copy-start.2 = (f32[12,512]{1,0:T(8,128)S(1)}, f32[12,512]{1,0:T(8,128)}, u32[]{:S(2)}) copy-start(f32[12,512]{1,0:T(8,128)} %param.14) | copy-start | bytes 73732
  6.5 16.9 %copy-start.3 = (f32[12,32]{1,0:T(8,128)S(1)}, f32[12,32]{1,0:T(8,128)}, u32[]{:S(2)}) copy-start(f32[12,32]{1,0:T(8,128)} %param.15) | copy-start | bytes 4612
  6.5 17.2 %copy-start.7 = (s32[1,12]{1,0:T(1,128)S(1)}, s32[1,12]{1,0:T(1,128)}, u32[]{:S(2)}) copy-start(s32[1,12]{1,0:T(1,128)} %param.9) | copy-start | bytes 148
  6.5 17.5 %copy-start.5 = (s32[4,12]{1,0:T(4,128)S(1)}, s32[4,12]{1,0:T(4,128)}, u32[]{:S(2)}) copy-start(s32[4,12]{1,0:T(4,128)} %param.10) | copy-start | bytes 580
  8.3 32.9 %collective-permute-start = (f32[2,32,512]{2,1,0:T(8,128)}, f32[2,32,512]{2,1,0:T(8,128)}, u32[]{:S(2)}, u32[]{:S(2)}) collective-permute-start(f32[2,32,512]{2,1,0:T(8,128)} %get-tuple-element.14), channel_id=1, source_target_pairs={{0,1},{1,2},{2,3},{4,5},{5,6},{6,7},{8,9},{9,10},{10,11},{12,13},{... | collective-permute-start | bytes 393224 | tf_op jit(solution)/shard_map/ppermute | solution.py:19
  13.9 28.4 %collective-permute-start.1 = (f32[2,32,512]{2,1,0:T(8,128)}, f32[2,32,512]{2,1,0:T(8,128)}, u32[]{:S(2)}, u32[]{:S(2)}) collective-permute-start(f32[2,32,512]{2,1,0:T(8,128)} %get-tuple-element.13), channel_id=1, source_target_pairs={{1,0},{2,1},{3,2},{5,4},{6,5},{7,6},{9,8},{10,9},{11,10},{13,12},{... | collective-permute-start | bytes 393224 | tf_op jit(solution)/shard_map/ppermute | solution.py:22
  16.3 12.6 %collective-permute-start.2 = (f32[32,16,2]{2,1,0:T(8,128)S(1)}, f32[32,16,2]{2,1,0:T(8,128)S(1)}, u32[]{:S(2)}, u32[]{:S(2)}) collective-permute-start(f32[32,16,2]{2,1,0:T(8,128)S(1)} %get-tuple-element.15), channel_id=1, source_target_pairs={{0,1},{1,2},{2,3},{4,5},{5,6},{6,7},{8,9},{9,10},{10,11},{12,13},{... | collective-permute-start | bytes 12296 | tf_op jit(solution)/shard_map/ppermute | solution.py:19
  20.9 9.1 %collective-permute-start.3 = (f32[32,16,2]{2,1,0:T(8,128)S(1)}, f32[32,16,2]{2,1,0:T(8,128)S(1)}, u32[]{:S(2)}, u32[]{:S(2)}) collective-permute-start(f32[32,16,2]{2,1,0:T(8,128)S(1)} %get-tuple-element.16), channel_id=1, source_target_pairs={{1,0},{2,1},{3,2},{5,4},{6,5},{7,6},{9,8},{10,9},{11,10},{13,12},{... | collective-permute-start | bytes 12296 | tf_op jit(solution)/shard_map/ppermute | solution.py:22
  24.3 5.7 %copy-start = (f32[32,16,64]{2,1,0:T(8,128)S(1)}, f32[32,16,64]{2,1,0:T(8,128)}, u32[]{:S(2)}) copy-start(f32[32,16,64]{2,1,0:T(8,128)} %param.17) | copy-start | bytes 393220
  36.7 5.5 %copy-start.1 = (f32[16,32,512]{2,1,0:T(8,128)S(1)}, f32[16,32,512]{2,1,0:T(8,128)}, u32[]{:S(2)}) copy-start(f32[16,32,512]{2,1,0:T(8,128)} %param.16) | copy-start | bytes 3145732
  139.2 5.9 %copy-start.6 = (s32[4]{0:T(128)S(1)}, s32[4]{0:T(128)}, u32[]{:S(2)}) copy-start(s32[4]{0:T(128)} %param.12) | copy-start | bytes 52
  140.2 10.9 %all-to-all-start = ((f32[4,1,8192]{2,1,0:T(1,128)}), f32[4,1,8192]{2,1,0:T(1,128)S(1)}, u32[]{:S(2)}, u32[]{:S(2)}) async-start(f32[4,1,8192]{2,1,0:T(1,128)} %reshape.59), calls=%async_computation | async-start | bytes 262144 | tf_op jit(solution)/shard_map/all_to_all | solution.py:192
  145.1 41.2 %reduce-scatter.2.cloned.1.call-start = ((), (), s32[]{:S(2)}) async-start(), calls=%async_computation.2 | async-start | bytes 294912 | tf_op jit(solution)/shard_map/reduce_scatter | solution.py:198
Sparse Core Ops, SparseCore 0:
  153.5 32.7 reduce-scatter.1
